TPU v7x, 256 devices: a whole 4x4x8 slice. The times are simulated.
256 devices in a mesh: expert: 64 (over z, x, core), tensor: 4 (over y).
Axes of the slice: x: 4, y: 4, z: 8, core: 2. Of those that a mesh axis runs over, the one named last changes fastest.
Arguments:
- tokens: bfloat16 [16384, 2048], P('expert', 'tensor'), may hold values from -6 to 6
- out_grads: bfloat16 [16384, 2048], P('expert', 'tensor'), may hold values from -6 to 6
- species: int32 [16384, 1], P('expert'), may hold values from 0 to 63; in each aligned block of 64 rows (0 to 63, 64 to 127, ...) at most 2 rows name the same one
- expert_table: int32 [64], replicated, may hold values from 0 to 63, each once
- gate_weight: bfloat16 [64, 2048, 4096], P('expert', None, 'tensor'), may hold values from -0.125 to 0.125
- up_weight: bfloat16 [64, 2048, 4096], P('expert', None, 'tensor'), may hold values from -0.125 to 0.125
- down_weight: bfloat16 [64, 4096, 2048], P('expert', 'tensor'), may hold values from -0.09375 to 0.09375
Outputs:
- token_grads: bfloat16 [16384, 2048], P('expert', 'tensor')
Inputs may be any that keep to these rules, and one draw needn't show every extreme that they name: In each aligned block of 64 rows no species occurs more than 2 times, and in some blocks one species occurs exactly 2 times. `expert_table`: each species has a different expert.
All inputs are finite; a program needn't handle non-finite values.
Results may differ from a plain program's by a relative error of at most 0.0095.
Values may be sent and summed in bfloat16 or wider, within the bound.
A program may use at most 64 MiB of HBM per device.

v0:
```python
import jax
import jax.numpy as jnp
from jax import lax
from jax.sharding import PartitionSpec as P


def expert_partial(expert_rows, expert_grads, gate_matrix, up_matrix, down_matrix):
    contract = (((1,), (1,)), ((), ()))
    gate_pre = jnp.dot(expert_rows, gate_matrix, preferred_element_type=jnp.float32)
    up_pre = jnp.dot(expert_rows, up_matrix, preferred_element_type=jnp.float32)
    hidden_grad = lax.dot_general(
        expert_grads, down_matrix, contract, preferred_element_type=jnp.float32
    )
    sigmoid_gate = jax.nn.sigmoid(gate_pre)
    up_grad = (hidden_grad * gate_pre * sigmoid_gate).astype(jnp.bfloat16)
    gate_grad = (
        hidden_grad * up_pre * sigmoid_gate * (1.0 + gate_pre * (1.0 - sigmoid_gate))
    ).astype(jnp.bfloat16)
    partial_sum = lax.dot_general(
        gate_grad, gate_matrix, contract, preferred_element_type=jnp.float32
    )
    return partial_sum + lax.dot_general(
        up_grad, up_matrix, contract, preferred_element_type=jnp.float32
    )


def per_device(tokens, out_grads, species, expert_table, gate_weight, up_weight, down_weight):
    tensor_size = lax.axis_size("tensor")
    tensor_index = lax.axis_index("tensor")
    experts = expert_table.shape[0]
    group_tokens_count = tokens.shape[0]
    rows_dev = group_tokens_count // tensor_size
    head_width = tokens.shape[1]
    model_width = head_width * tensor_size
    capacity = 2 * rows_dev // experts
    expert_ids = jnp.arange(experts, dtype=jnp.int32)
    species_hits = species == expert_ids[None, :]
    expert_of = jnp.sum(jnp.where(species_hits, expert_table[None, :], 0), axis=1).reshape(
        tensor_size, rows_dev
    )
    onehot = (expert_of[:, :, None] == expert_ids[None, None, :]).astype(jnp.int32)
    earlier = jnp.cumsum(onehot, axis=1) - onehot
    slot_of = jnp.sum(earlier * onehot, axis=2)
    place_of = expert_of * capacity + slot_of
    slot_ids = jnp.arange(experts * capacity, dtype=jnp.int32)
    select = (slot_ids[None, :, None] == place_of[:, None, :]).astype(jnp.bfloat16)
    group_select = select.reshape(tensor_size, experts, capacity, rows_dev)
    own_select = lax.dynamic_index_in_dim(select, tensor_index, 0, keepdims=False)
    group_tokens, group_grads = (
        lax.all_gather(tokens, "tensor", axis=1, tiled=True),
        lax.all_gather(out_grads, "tensor", axis=1, tiled=True),
    )
    packed_rows = jnp.einsum(
        "tecr,trd->etcd",
        group_select,
        group_tokens.reshape(tensor_size, rows_dev, model_width),
        preferred_element_type=jnp.float32,
    ).astype(jnp.bfloat16)
    packed_grads = jnp.einsum(
        "tecr,trd->etcd",
        group_select,
        group_grads.reshape(tensor_size, rows_dev, model_width),
        preferred_element_type=jnp.float32,
    ).astype(jnp.bfloat16)
    packed_rows = packed_rows.reshape(experts, tensor_size * capacity, model_width)
    packed_grads = packed_grads.reshape(experts, tensor_size * capacity, model_width)
    expert_rows, expert_grads = (
        lax.all_to_all(packed_rows, "expert", split_axis=0, concat_axis=0, tiled=True),
        lax.all_to_all(packed_grads, "expert", split_axis=0, concat_axis=0, tiled=True),
    )
    slot_count = expert_rows.shape[0] * expert_rows.shape[1]
    partial_sum = expert_partial(
        expert_rows.reshape(slot_count, model_width),
        expert_grads.reshape(slot_count, model_width),
        gate_weight[0],
        up_weight[0],
        down_weight[0],
    )
    summed = lax.psum_scatter(
        partial_sum.reshape(experts, tensor_size * capacity, model_width).astype(jnp.bfloat16),
        "tensor",
        scatter_dimension=1,
        tiled=True,
    )
    returned = lax.all_to_all(summed, "expert", split_axis=0, concat_axis=0, tiled=True)
    own_grads = lax.dot_general(
        own_select,
        returned.reshape(experts * capacity, model_width),
        (((0,), (0,)), ((), ())),
        preferred_element_type=jnp.float32,
    ).astype(jnp.bfloat16)
    token_grads = lax.all_to_all(own_grads, "tensor", split_axis=1, concat_axis=0, tiled=True)
    return token_grads


def solution(mesh):
    placed = (
        P("expert", "tensor"),
        P("expert", "tensor"),
        P("expert", None),
        P(),
        P("expert", None, "tensor"),
        P("expert", None, "tensor"),
        P("expert", "tensor", None),
    )
    return jax.shard_map(
        per_device, mesh=mesh, in_specs=placed, out_specs=P("expert", "tensor"), check_vma=False
    )
```

profile of v0, /device:TPU:1, one launch (start us, length us, event | category | flops | bytes accessed | tf_op | source)
XLA Modules:
  0.0 264.5 jit_solution(15965972787222262756)
XLA Ops:
  6.5 0.7 all-gather.3.cloned.1.call-update
  7.3 0.8 select_reduce_fusion.1
  8.6 28.9 %all-gather.3.cloned.1.call-done = bf16[256,2048]{1,0:T(8,128)(2,1)} async-done(((bf16[256,512]{1,0:T(8,128)(2,1)}), bf16[256,2048]{1,0:T(8,128)(2,1)}) %all-gather.3.cloned.1.call-update) | async-done | bytes 1048592 | tf_op jit(solution)/shard_map/all_gather | solution.py:51
  37.6 2.0 convolution_convert_fusion.1
  39.5 2.5 copy.26
  42.0 12.7 %all-to-all-start = ((bf16[64,8,2048]{2,1,0:T(8,128)(2,1)}), bf16[64,8,2048]{2,1,0:T(8,128)(2,1)S(1)}, u32[]{:S(2)}, u32[]{:S(2)}) async-start(bf16[64,8,2048]{2,1,0:T(8,128)(2,1)} %copy.26), calls=%async_computation | async-start | bytes 4194304 | tf_op jit(solution)/shard_map/all_to_all | solution.py:69
  54.8 0.7 all-gather.5.cloned.1.call-update
  55.5 26.7 %all-gather.5.cloned.1.call-done = bf16[256,2048]{1,0:T(8,128)(2,1)} async-done(((bf16[256,512]{1,0:T(8,128)(2,1)}), bf16[256,2048]{1,0:T(8,128)(2,1)}) %all-gather.5.cloned.1.call-update) | async-done | bytes 1048592 | tf_op jit(solution)/shard_map/all_gather | solution.py:50
  82.2 2.0 convolution_convert_fusion
  84.2 2.5 copy.27
  86.6 17.8 %all-to-all-done = bf16[64,8,2048]{2,1,0:T(8,128)(2,1)S(1)} async-done(((bf16[64,8,2048]{2,1,0:T(8,128)(2,1)}), bf16[64,8,2048]{2,1,0:T(8,128)(2,1)S(1)}, u32[]{:S(2)}, u32[]{:S(2)}) %all-to-all-start) | async-done | bytes 2097184 | tf_op jit(solution)/shard_map/all_to_all | solution.py:69
  104.4 7.2 %all-to-all-start.1 = ((bf16[64,8,2048]{2,1,0:T(8,128)(2,1)}), bf16[64,8,2048]{2,1,0:T(8,128)(2,1)}, u32[]{:S(2)}, u32[]{:S(2)}) async-start(bf16[64,8,2048]{2,1,0:T(8,128)(2,1)} %copy.27), calls=%async_computation.1 | async-start | bytes 4194304 | tf_op jit(solution)/shard_map/all_to_all | solution.py:68
  111.8 6.0 %fusion.8 = f32[512,1024]{1,0:T(8,128)} fusion(bf16[1,1024,2048]{2,1,0:T(8,128)(2,1)} %param.13, bf16[64,8,2048]{2,1,0:T(8,128)(2,1)S(1)} %all-to-all-done), kind=kOutput, calls=%fused_computation.8 | convolution fusion | flops 2147483648 | bytes 8388608 | tf_op jit(solution)/shard_map/dot_general | solution.py:11
  117.8 43.4 %all-to-all-done.1 = bf16[64,8,2048]{2,1,0:T(8,128)(2,1)} async-done(((bf16[64,8,2048]{2,1,0:T(8,128)(2,1)}), bf16[64,8,2048]{2,1,0:T(8,128)(2,1)}, u32[]{:S(2)}, u32[]{:S(2)}) %all-to-all-start.1) | async-done | bytes 2097184 | tf_op jit(solution)/shard_map/all_to_all | solution.py:68
  161.2 6.5 %fusion.2 = f32[512,1024]{1,0:T(8,128)} fusion(bf16[1,2048,1024]{2,1,0:T(8,128)(2,1)} %param.11, bf16[64,8,2048]{2,1,0:T(8,128)(2,1)} %all-to-all-done.1), kind=kOutput, calls=%fused_computation.2 | convolution fusion | flops 2147483648 | bytes 8388608 | tf_op jit(solution)/shard_map/dot_general | solution.py:9
  167.7 11.5 %fusion = f32[512,2048]{1,0:T(8,128)} fusion(bf16[1,2048,1024]{2,1,0:T(8,128)(2,1)} %param.11, f32[512,1024]{1,0:T(8,128)} %fusion.2, f32[512,1024]{1,0:T(8,128)S(1)} %copy-done, bf16[1,2048,1024]{2,1,0:T(8,128)(2,1)} %param.12, bf16[64,8,2048]{2,1,0:T(8,128)(2,1)} %all-to-all-done.1), kind=kOutput, calls=%fused_computation | convolution fusion | flops 4300210176 | bytes 18874368 | tf_op jit(solution)/shard_map/dot_general | solution.py:19
  179.2 6.5 %fusion.12 = bf16[64,8,2048]{2,1,0:T(8,128)(2,1)S(1)} fusion(f32[512,2048]{1,0:T(8,128)} %fusion, bf16[1,2048,1024]{2,1,0:T(8,128)(2,1)} %param.12, f32[512,1024]{1,0:T(8,128)S(1)} %copy-done, f32[512,1024]{1,0:T(8,128)} %fusion.2), kind=kOutput, calls=%fused_computation.13 | convolution fusion | flops 2152726528 | bytes 14680064 | tf_op jit(solution)/shard_map/dot_general | solution.py:22
  185.7 2.5 copy.28
  188.2 29.1 %reduce-scatter.2.cloned.1.call-done = bf16[64,2,2048]{2,0,1:T(8,128)(2,1)} async-done(((bf16[64,8,2048]{2,0,1:T(8,128)(2,1)}), bf16[64,2,2048]{2,0,1:T(8,128)(2,1)}) %reduce-scatter.2.cloned.1.call-update) | async-done | bytes 524304 | tf_op jit(solution)/shard_map/reduce_scatter | solution.py:79
  217.3 2.4 copy.29
  219.7 10.7 %all-to-all-start.2 = ((bf16[64,2,2048]{2,1,0:T(2,128)(2,1)}), bf16[64,2,2048]{2,1,0:T(2,128)(2,1)S(1)}, u32[]{:S(2)}, u32[]{:S(2)}) async-start(bf16[64,2,2048]{2,1,0:T(2,128)(2,1)} %copy.29), calls=%async_computation.3 | async-start | bytes 1048576 | tf_op jit(solution)/shard_map/all_to_all | solution.py:85
  230.4 17.7 %all-to-all-done.2 = bf16[64,2,2048]{2,1,0:T(2,128)(2,1)S(1)} async-done(((bf16[64,2,2048]{2,1,0:T(2,128)(2,1)}), bf16[64,2,2048]{2,1,0:T(2,128)(2,1)S(1)}, u32[]{:S(2)}, u32[]{:S(2)}) %all-to-all-start.2) | async-done | bytes 524320 | tf_op jit(solution)/shard_map/all_to_all | solution.py:85
  248.6 8.6 %all_to_all.34 = bf16[64,4,512]{2,0,1:T(8,128)(2,1)S(1)} all-to-all(bf16[64,4,512]{2,0,1:T(8,128)(2,1)S(1)} %bitcast.69), channel_id=1, replica_groups=mesh['expert'=64,'tensor'=4] {'tensor'}, dimensions={1} | all-to-all | bytes 524288 | tf_op jit(solution)/shard_map/all_to_all | solution.py:92
  257.2 0.7 copy.37
  (16 shorter events, 1.3 us)
Async XLA Ops:
  6.5 31.0 %all-gather.3.cloned.1.call-start = ((), (), s32[]{:S(2)}) async-start(), calls=%async_computation.5 | async-start | bytes 1310720 | tf_op jit(solution)/shard_map/all_gather | solution.py:51
  42.0 62.4 %all-to-all-start = ((bf16[64,8,2048]{2,1,0:T(8,128)(2,1)}), bf16[64,8,2048]{2,1,0:T(8,128)(2,1)S(1)}, u32[]{:S(2)}, u32[]{:S(2)}) async-start(bf16[64,8,2048]{2,1,0:T(8,128)(2,1)} %copy.26), calls=%async_computation | async-start | bytes 4194304 | tf_op jit(solution)/shard_map/all_to_all | solution.py:69
  54.7 27.4 %all-gather.5.cloned.1.call-start = ((), (), s32[]{:S(2)}) async-start(), calls=%async_computation.6 | async-start | bytes 1310720 | tf_op jit(solution)/shard_map/all_gather | solution.py:50
  104.4 56.8 %all-to-all-start.1 = ((bf16[64,8,2048]{2,1,0:T(8,128)(2,1)}), bf16[64,8,2048]{2,1,0:T(8,128)(2,1)}, u32[]{:S(2)}, u32[]{:S(2)}) async-start(bf16[64,8,2048]{2,1,0:T(8,128)(2,1)} %copy.27), calls=%async_computation.1 | async-start | bytes 4194304 | tf_op jit(solution)/shard_map/all_to_all | solution.py:68
  111.6 105.7 %reduce-scatter.2.cloned.1.call-start = ((), (), s32[]{:S(2)}) async-start(), calls=%async_computation.7 | async-start | bytes 2621440 | tf_op jit(solution)/shard_map/reduce_scatter | solution.py:79
  117.8 49.9 %copy-start = (f32[512,1024]{1,0:T(8,128)S(1)}, f32[512,1024]{1,0:T(8,128)}, u32[]{:S(2)}) copy-start(f32[512,1024]{1,0:T(8,128)} %fusion.8) | copy-start | bytes 6291460
  219.7 28.4 %all-to-all-start.2 = ((bf16[64,2,2048]{2,1,0:T(2,128)(2,1)}), bf16[64,2,2048]{2,1,0:T(2,128)(2,1)S(1)}, u32[]{:S(2)}, u32[]{:S(2)}) async-start(bf16[64,2,2048]{2,1,0:T(2,128)(2,1)} %copy.29), calls=%async_computation.3 | async-start | bytes 1048576 | tf_op jit(solution)/shard_map/all_to_all | solution.py:85
Sparse Core Ops, SparseCore 0:
  9.1 28.3 all-gather.2
  57.4 24.7 all-gather.4
  188.4 28.8 reduce-scatter.1
where the time goes:
time: 265 us; the launch traced here: 264 us
  waiting for transfers between devices  165 us (62%)
  matrix products  34.7 us (13%)
  starting transfers between devices  30.9 us (12%)
  between operations  13.2 us (5%)
  local copies, waits for them, and re-layouts  10.8 us (4%)
  blocking collectives  8.61 us (3%)
    all_to_all x1, waiting for transfers between devices, per_device(): lax.all_to_all(packed_rows, 'expert', split_axis=0, concat_axis=0, tiled=...  43.4 us
    reduce_scatter x1, waiting for transfers between devices, per_device(): lax.psum_scatter(partial_sum.reshape(experts, tensor_size * capacity, mod...  29.1 us
    all_gather x1, waiting for transfers between devices, per_device(): lax.all_gather(out_grads, 'tensor', axis=1, tiled=True)  28.9 us
    all_gather x1, waiting for transfers between devices, per_device(): lax.all_gather(tokens, 'tensor', axis=1, tiled=True)  26.7 us
    all_to_all x1, waiting for transfers between devices, per_device(): lax.all_to_all(packed_grads, 'expert', split_axis=0, concat_axis=0, tiled...  17.8 us
    all_to_all x1, waiting for transfers between devices, per_device(): lax.all_to_all(summed, 'expert', split_axis=0, concat_axis=0, tiled=True)  17.7 us
    all_to_all x1, starting transfers between devices, per_device(): lax.all_to_all(packed_grads, 'expert', split_axis=0, concat_axis=0, tiled...  12.7 us
    dot_general x1, matrix products, expert_partial(): lax.dot_general(gate_grad, gate_matrix, contract, preferred_element_type=...  11.5 us
  transfers between devices with their start and end apart: 6, of which 6 were waited for; matrix products, arithmetic and copies ran while one was open for 4% of the time, Pallas kernels for 0%

commit v1 on v0

--- a/solution.py
+++ b/solution.py
@@ -48,7 +48,9 @@
     own_select = lax.dynamic_index_in_dim(select, tensor_index, 0, keepdims=False)
     group_tokens, group_grads = (
         lax.all_gather(tokens, "tensor", axis=1, tiled=True),
-        lax.all_gather(out_grads, "tensor", axis=1, tiled=True),
+        jnp.concatenate(
+            lax.all_to_all(jnp.stack([out_grads] * lax.axis_size("tensor")), "tensor", 0, 0), axis=1
+        ),
     )
     packed_rows = jnp.einsum(
         "tecr,trd->etcd",

time: 265 us -> 256 us (0.966)
  waiting for transfers between devices: 165 us -> 147 us
  starting transfers between devices: 30.9 us -> 37.2 us
  local copies, waits for them, and re-layouts: 10.8 us -> 14.5 us
    all_gather x1 -> x0, waiting for transfers between devices: 28.9 us -> none  [per_device(): lax.all_gather(out_grads, 'tensor', axis=1, tiled=True)]
    all_to_all x0 -> x1, waiting for transfers between devices: none -> 12.8 us  [per_device(): lax.all_to_all(jnp.stack([out_grads] * lax.axis_size('tensor')), 'tensor'...]
    all_to_all x0 -> x1, starting transfers between devices: none -> 5 us  [per_device(): lax.all_to_all(jnp.stack([out_grads] * lax.axis_size('tensor')), 'tensor'...]
    another operation x0 -> x2, local copies, waits for them, and re-layouts: none -> 2.84 us  [the longest x1 2.03 us: per_device(): jnp.stack([out_grads] * lax.axis_size('tensor'))]
where the time goes in v1:
time: 256 us; the launch traced here: 255 us
  waiting for transfers between devices  147 us (57%)
  starting transfers between devices  37.2 us (15%)
  matrix products  33.5 us (13%)
  local copies, waits for them, and re-layouts  14.5 us (6%)
  between operations  13.5 us (5%)
  blocking collectives  8.59 us (3%)
    all_to_all x1, waiting for transfers between devices, per_device(): lax.all_to_all(packed_rows, 'expert', split_axis=0, concat_axis=0, tiled=...  43.4 us
    reduce_scatter x1, waiting for transfers between devices, per_device(): lax.psum_scatter(partial_sum.reshape(experts, tensor_size * capacity, mod...  28.1 us
    all_gather x1, waiting for transfers between devices, per_device(): lax.all_gather(tokens, 'tensor', axis=1, tiled=True)  25.8 us
    all_to_all x1, waiting for transfers between devices, per_device(): lax.all_to_all(packed_grads, 'expert', split_axis=0, concat_axis=0, tiled...  18.7 us
    all_to_all x1, waiting for transfers between devices, per_device(): lax.all_to_all(summed, 'expert', split_axis=0, concat_axis=0, tiled=True)  17.7 us
    all_to_all x1, starting transfers between devices, per_device(): lax.all_to_all(packed_grads, 'expert', split_axis=0, concat_axis=0, tiled...  14 us
    all_to_all x1, waiting for transfers between devices, per_device(): lax.all_to_all(jnp.stack([out_grads] * lax.axis_size('tensor')), 'tensor'...  12.8 us
    dot_general x1, matrix products, expert_partial(): lax.dot_general(gate_grad, gate_matrix, contract, preferred_element_type=...  11.5 us
  transfers between devices with their start and end apart: 6, of which 6 were waited for; matrix products, arithmetic and copies ran while one was open for 4% of the time, Pallas kernels for 0%

profile of v1, /device:TPU:1, one launch (start us, length us, event | category | flops | bytes accessed | tf_op | source)
XLA Modules:
  0.0 255.0 jit_solution(17632165577815202470)
XLA Ops:
  6.5 2.0 stack.2
  8.6 5.0 %all-to-all-start = ((bf16[4,256,512]{2,1,0:T(8,128)(2,1)}), bf16[4,256,512]{2,1,0:T(8,128)(2,1)S(1)}, u32[]{:S(2)}, u32[]{:S(2)}) async-start(bf16[4,256,512]{2,1,0:T(8,128)(2,1)} %stack.2), calls=%async_computation | async-start | bytes 2097152 | tf_op jit(solution)/shard_map/all_to_all | solution.py:52
  14.2 12.8 %all-to-all-done = bf16[4,256,512]{2,1,0:T(8,128)(2,1)S(1)} async-done(((bf16[4,256,512]{2,1,0:T(8,128)(2,1)}), bf16[4,256,512]{2,1,0:T(8,128)(2,1)S(1)}, u32[]{:S(2)}, u32[]{:S(2)}) %all-to-all-start) | async-done | bytes 1048608 | tf_op jit(solution)/shard_map/all_to_all | solution.py:52
  27.1 0.8 copy.29
  27.9 0.8 reshape.51
  28.7 0.8 convolution_convert_fusion.1
  29.5 2.5 copy.30
  31.9 14.0 %all-to-all-start.1 = ((bf16[64,8,2048]{2,1,0:T(8,128)(2,1)}), bf16[64,8,2048]{2,1,0:T(8,128)(2,1)S(1)}, u32[]{:S(2)}, u32[]{:S(2)}) async-start(bf16[64,8,2048]{2,1,0:T(8,128)(2,1)} %copy.30), calls=%async_computation.1 | async-start | bytes 4194304 | tf_op jit(solution)/shard_map/all_to_all | solution.py:71
  46.7 25.8 %all-gather.2.cloned.1.call-done = bf16[256,2048]{1,0:T(8,128)(2,1)} async-done(((bf16[256,512]{1,0:T(8,128)(2,1)}), bf16[256,2048]{1,0:T(8,128)(2,1)}) %all-gather.2.cloned.1.call-update) | async-done | bytes 1048592 | tf_op jit(solution)/shard_map/all_gather | solution.py:50
  72.5 2.0 convolution_convert_fusion
  74.5 2.5 copy.31
  76.9 18.7 %all-to-all-done.1 = bf16[64,8,2048]{2,1,0:T(8,128)(2,1)S(1)} async-done(((bf16[64,8,2048]{2,1,0:T(8,128)(2,1)}), bf16[64,8,2048]{2,1,0:T(8,128)(2,1)S(1)}, u32[]{:S(2)}, u32[]{:S(2)}) %all-to-all-start.1) | async-done | bytes 2097184 | tf_op jit(solution)/shard_map/all_to_all | solution.py:71
  95.7 7.2 %all-to-all-start.2 = ((bf16[64,8,2048]{2,1,0:T(8,128)(2,1)}), bf16[64,8,2048]{2,1,0:T(8,128)(2,1)}, u32[]{:S(2)}, u32[]{:S(2)}) async-start(bf16[64,8,2048]{2,1,0:T(8,128)(2,1)} %copy.31), calls=%async_computation.2 | async-start | bytes 4194304 | tf_op jit(solution)/shard_map/all_to_all | solution.py:70
  103.0 6.0 %fusion.8 = f32[512,1024]{1,0:T(8,128)} fusion(bf16[1,1024,2048]{2,1,0:T(8,128)(2,1)} %param.13, bf16[64,8,2048]{2,1,0:T(8,128)(2,1)S(1)} %all-to-all-done.1), kind=kOutput, calls=%fused_computation.8 | convolution fusion | flops 2147483648 | bytes 8388608 | tf_op jit(solution)/shard_map/dot_general | solution.py:11
  109.0 43.4 %all-to-all-done.2 = bf16[64,8,2048]{2,1,0:T(8,128)(2,1)} async-done(((bf16[64,8,2048]{2,1,0:T(8,128)(2,1)}), bf16[64,8,2048]{2,1,0:T(8,128)(2,1)}, u32[]{:S(2)}, u32[]{:S(2)}) %all-to-all-start.2) | async-done | bytes 2097184 | tf_op jit(solution)/shard_map/all_to_all | solution.py:70
  152.4 6.5 %fusion.2 = f32[512,1024]{1,0:T(8,128)} fusion(bf16[1,2048,1024]{2,1,0:T(8,128)(2,1)} %param.11, bf16[64,8,2048]{2,1,0:T(8,128)(2,1)} %all-to-all-done.2), kind=kOutput, calls=%fused_computation.2 | convolution fusion | flops 2147483648 | bytes 8388608 | tf_op jit(solution)/shard_map/dot_general | solution.py:9
  158.9 11.5 %fusion = f32[512,2048]{1,0:T(8,128)} fusion(bf16[1,2048,1024]{2,1,0:T(8,128)(2,1)} %param.11, f32[512,1024]{1,0:T(8,128)} %fusion.2, f32[512,1024]{1,0:T(8,128)S(1)} %copy-done.2, bf16[1,2048,1024]{2,1,0:T(8,128)(2,1)} %param.12, bf16[64,8,2048]{2,1,0:T(8,128)(2,1)} %all-to-all-done.2), kind=kOutput, calls=%fused_computation | convolution fusion | flops 4300210176 | bytes 18874368 | tf_op jit(solution)/shard_map/dot_general | solution.py:19
  170.5 6.5 %fusion.12 = bf16[64,8,2048]{2,1,0:T(8,128)(2,1)S(1)} fusion(f32[512,2048]{1,0:T(8,128)} %fusion, bf16[1,2048,1024]{2,1,0:T(8,128)(2,1)} %param.12, f32[512,1024]{1,0:T(8,128)S(1)} %copy-done.2, f32[512,1024]{1,0:T(8,128)} %fusion.2), kind=kOutput, calls=%fused_computation.13 | convolution fusion | flops 2152726528 | bytes 14680064 | tf_op jit(solution)/shard_map/dot_general | solution.py:22
  177.0 2.5 copy.32
  179.5 28.1 %reduce-scatter.2.cloned.1.call-done = bf16[64,2,2048]{2,0,1:T(8,128)(2,1)} async-done(((bf16[64,8,2048]{2,0,1:T(8,128)(2,1)}), bf16[64,2,2048]{2,0,1:T(8,128)(2,1)}) %reduce-scatter.2.cloned.1.call-update) | async-done | bytes 524304 | tf_op jit(solution)/shard_map/reduce_scatter | solution.py:81
  207.6 2.4 copy.33
  210.0 10.7 %all-to-all-start.3 = ((bf16[64,2,2048]{2,1,0:T(2,128)(2,1)}), bf16[64,2,2048]{2,1,0:T(2,128)(2,1)S(1)}, u32[]{:S(2)}, u32[]{:S(2)}) async-start(bf16[64,2,2048]{2,1,0:T(2,128)(2,1)} %copy.33), calls=%async_computation.4 | async-start | bytes 1048576 | tf_op jit(solution)/shard_map/all_to_all | solution.py:87
  220.7 17.7 %all-to-all-done.3 = bf16[64,2,2048]{2,1,0:T(2,128)(2,1)S(1)} async-done(((bf16[64,2,2048]{2,1,0:T(2,128)(2,1)}), bf16[64,2,2048]{2,1,0:T(2,128)(2,1)S(1)}, u32[]{:S(2)}, u32[]{:S(2)}) %all-to-all-start.3) | async-done | bytes 524320 | tf_op jit(solution)/shard_map/all_to_all | solution.py:87
  238.9 8.6 %all_to_all.39 = bf16[64,4,512]{2,0,1:T(8,128)(2,1)S(1)} all-to-all(bf16[64,4,512]{2,0,1:T(8,128)(2,1)S(1)} %bitcast.67), channel_id=1, replica_groups=mesh['expert'=64,'tensor'=4] {'tensor'}, dimensions={1} | all-to-all | bytes 524288 | tf_op jit(solution)/shard_map/all_to_all | solution.py:94
  (22 shorter events, 2.8 us)
Async XLA Ops:
  6.5 7.0 %copy-start.1 = (s32[64]{0:T(128)S(1)}, s32[64]{0:T(128)}, u32[]{:S(2)}) copy-start(s32[64]{0:T(128)} %param.10) | copy-start | bytes 772
  6.5 7.0 %copy-start = (s32[256,1]{0,1:T(1,128)S(1)}, s32[256,1]{0,1:T(1,128)}, u32[]{:S(2)}) copy-start(s32[256,1]{0,1:T(1,128)} %param.9) | copy-start | bytes 3076
  8.6 18.5 %all-to-all-start = ((bf16[4,256,512]{2,1,0:T(8,128)(2,1)}), bf16[4,256,512]{2,1,0:T(8,128)(2,1)S(1)}, u32[]{:S(2)}, u32[]{:S(2)}) async-start(bf16[4,256,512]{2,1,0:T(8,128)(2,1)} %stack.2), calls=%async_computation | async-start | bytes 2097152 | tf_op jit(solution)/shard_map/all_to_all | solution.py:52
  31.9 63.7 %all-to-all-start.1 = ((bf16[64,8,2048]{2,1,0:T(8,128)(2,1)}), bf16[64,8,2048]{2,1,0:T(8,128)(2,1)S(1)}, u32[]{:S(2)}, u32[]{:S(2)}) async-start(bf16[64,8,2048]{2,1,0:T(8,128)(2,1)} %copy.30), calls=%async_computation.1 | async-start | bytes 4194304 | tf_op jit(solution)/shard_map/all_to_all | solution.py:71
  46.0 26.5 %all-gather.2.cloned.1.call-start = ((), (), s32[]{:S(2)}) async-start(), calls=%async_computation.6 | async-start | bytes 1310720 | tf_op jit(solution)/shard_map/all_gather | solution.py:50
  95.7 56.8 %all-to-all-start.2 = ((bf16[64,8,2048]{2,1,0:T(8,128)(2,1)}), bf16[64,8,2048]{2,1,0:T(8,128)(2,1)}, u32[]{:S(2)}, u32[]{:S(2)}) async-start(bf16[64,8,2048]{2,1,0:T(8,128)(2,1)} %copy.31), calls=%async_computation.2 | async-start | bytes 4194304 | tf_op jit(solution)/shard_map/all_to_all | solution.py:70
  102.8 104.8 %reduce-scatter.2.cloned.1.call-start = ((), (), s32[]{:S(2)}) async-start(), calls=%async_computation.7 | async-start | bytes 2621440 | tf_op jit(solution)/shard_map/reduce_scatter | solution.py:81
  109.0 49.9 %copy-start.2 = (f32[512,1024]{1,0:T(8,128)S(1)}, f32[512,1024]{1,0:T(8,128)}, u32[]{:S(2)}) copy-start(f32[512,1024]{1,0:T(8,128)} %fusion.8) | copy-start | bytes 6291460
  210.0 28.4 %all-to-all-start.3 = ((bf16[64,2,2048]{2,1,0:T(2,128)(2,1)}), bf16[64,2,2048]{2,1,0:T(2,128)(2,1)S(1)}, u32[]{:S(2)}, u32[]{:S(2)}) async-start(bf16[64,2,2048]{2,1,0:T(2,128)(2,1)} %copy.33), calls=%async_computation.4 | async-start | bytes 1048576 | tf_op jit(solution)/shard_map/all_to_all | solution.py:87
Sparse Core Ops, SparseCore 0:
  48.6 23.8 all-gather.1
  179.6 27.9 reduce-scatter.1
